TPU v7x, 32 devices: a whole 2x2x4 slice. The times are simulated.
32 devices in a mesh: groups: 2 (over y), grid: 4 (over z), mesh: 2 (over x), sub: 2 (over core).
Axes of the slice: x: 2, y: 2, z: 4, core: 2. Of those that a mesh axis runs over, the one named last changes fastest.
Arguments:
- grid_feat: bfloat16 [8192, 256], P(('groups', 'grid')), parts along dimension 0, may hold values from -6 to 6
- mesh_state: bfloat16 [3072, 1024], P(('groups', 'grid'), ('mesh', 'sub')), parts along dimension 0, may hold values from -6 to 6
- embed_weight: bfloat16 [256, 1024], P(None, ('mesh', 'sub')), may hold values from -0.375 to 0.375
- embed_gain: float32 [1024], P(('mesh', 'sub')), may hold values from 0.25 to 1.75
- enc_send_weight: bfloat16 [1024, 1024], P(None, ('mesh', 'sub')), may hold values from -0.1875 to 0.1875
- enc_recv_weight: bfloat16 [1024, 1024], P(None, ('mesh', 'sub')), may hold values from -0.1875 to 0.1875
- enc_bias: float32 [1024], P(('mesh', 'sub')), may hold values from -3 to 3
- enc_out_weight: bfloat16 [1024, 1024], P(None, ('mesh', 'sub')), may hold values from -0.1875 to 0.1875
- enc_gain: float32 [1024], P(('mesh', 'sub')), may hold values from 0.25 to 1.75
- proc_send_weight: bfloat16 [1024, 1024], P(None, ('mesh', 'sub')), may hold values from -0.1875 to 0.1875
- proc_recv_weight: bfloat16 [1024, 1024], P(None, ('mesh', 'sub')), may hold values from -0.1875 to 0.1875
- proc_bias: float32 [1024], P(('mesh', 'sub')), may hold values from -3 to 3
- proc_out_weight: bfloat16 [1024, 1024], P(None, ('mesh', 'sub')), may hold values from -0.1875 to 0.1875
- proc_gain: float32 [1024], P(('mesh', 'sub')), may hold values from 0.25 to 1.75
- dec_send_weight: bfloat16 [1024, 1024], P(None, ('mesh', 'sub')), may hold values from -0.1875 to 0.1875
- dec_recv_weight: bfloat16 [1024, 1024], P(None, ('mesh', 'sub')), may hold values from -0.1875 to 0.1875
- dec_bias: float32 [1024], P(('mesh', 'sub')), may hold values from -3 to 3
- dec_out_weight: bfloat16 [1024, 1024], P(None, ('mesh', 'sub')), may hold values from -0.1875 to 0.1875
- dec_gain: float32 [1024], P(('mesh', 'sub')), may hold values from 0.25 to 1.75
- enc_src: int32 [24, 16], P('groups'), parts along dimension 0, may hold values from 0 to 31, as said below
- enc_count: int32 [24], P('groups'), parts along dimension 0, may hold values from 1 to 16
- proc_nbr: int32 [24, 6], P('groups'), parts along dimension 0, may hold values from 0 to 11, as said below
- dec_src: int32 [64, 3], P('groups'), parts along dimension 0, may hold values from 0 to 11, as said below
Outputs:
- grid_out: bfloat16 [8192, 1024], P(('groups', 'grid'), ('mesh', 'sub')), parts along dimension 0
- mesh_out: bfloat16 [3072, 1024], P(('groups', 'grid'), ('mesh', 'sub')), parts along dimension 0
There are 2 independent parts, one for each index of `groups`. A program takes and returns all parts, laid end to end along the dimension named above; an argument that names none is the same for every part. Nothing has to cross between parts.
Inputs may be any that keep to these rules, and one draw needn't show every extreme that they name: `enc_src`: entries of row m at positions k >= enc_count[m] are no edges. Take the 3 rows m with one and the same m // 3, and count their entries that name blocks b with one and the same b // 8: that count is never over 12, and in every such group of rows it equals 12 for some b // 8, counting only entries that are edges. `proc_nbr`: for mesh block m with o = m // 3, entries 0 and 1 name blocks b with b // 3 = (o - 1) mod 4, entries 2 and 3 with b // 3 = o, entries 4 and 5 with b // 3 = (o + 1) mod 4. `dec_src`: take the 8 rows g with one and the same g // 8, and count their entries that name blocks b with one and the same b // 3: that count is never over 6, and in every such group of rows it equals 6 for some b // 3.
All inputs are finite; a program needn't handle non-finite values.
Results may differ from a plain program's by a relative error of at most 0.014.
Values may be sent and summed in bfloat16 or wider, within the bound.
A program may use at most 64 MiB of HBM per device.

v0:
```python
import jax
import jax.numpy as jnp
from jax import lax
from jax.sharding import PartitionSpec as P

D = 1024
BLK = 128


EPSILON = 1e-05


def extended(cells, sides, width):
    for axis, dim in sides:
        count = lax.axis_size(axis)
        head = lax.slice_in_dim(cells, 0, width, axis=dim)
        tail = lax.slice_in_dim(cells, cells.shape[dim] - width, cells.shape[dim], axis=dim)
        cells = jnp.concatenate(
            [
                lax.ppermute(tail, axis, [(i, (i + 1) % count) for i in range(count)]),
                cells,
                lax.ppermute(head, axis, [((i + 1) % count, i) for i in range(count)]),
            ],
            axis=dim,
        )
    return cells


def normalize(partial_value, row_sum, row_squares, gain):
    row_mean = row_sum / D
    row_var = row_squares / D - row_mean * row_mean
    return (partial_value - row_mean[:, None]) * lax.rsqrt(row_var + EPSILON)[:, None] * gain


def norm_columns(partial_value, gain):
    row_sum, row_squares = lax.psum(
        (jnp.sum(partial_value, axis=1), jnp.sum(partial_value * partial_value, axis=1)),
        ("mesh", "sub"),
    )
    return normalize(partial_value, row_sum, row_squares, gain)


def fold_projection(weights, shard_piece):
    return tuple(
        (jnp.dot(shard_piece, weight, preferred_element_type=jnp.float32) for weight in weights)
    )


def fold_select(select_table, shard_piece):
    piece_count = shard_piece.shape[0]
    return jnp.dot(
        select_table, shard_piece.reshape(piece_count, -1), preferred_element_type=jnp.float32
    )


def block_table(sources, is_edge, block_total):
    block_ids = jnp.arange(block_total, dtype=jnp.int32)
    return ((sources[:, None] == block_ids[None, :]) & is_edge[:, None]).astype(jnp.bfloat16)


def edge_sum(picked, receiver, bias, edge_mask):
    block_count, fanout = edge_mask.shape
    gathered = picked.reshape((block_count, fanout) + receiver.shape[1:])
    active = jax.nn.silu(gathered + receiver[:, None] + bias) * edge_mask[:, :, None, None]
    return jnp.sum(active, axis=1).reshape(-1, receiver.shape[2]).astype(jnp.bfloat16)


def on_device(
    grid_feat,
    mesh_state,
    embed_weight,
    embed_gain,
    enc_send_weight,
    enc_recv_weight,
    enc_bias,
    enc_out_weight,
    enc_gain,
    proc_send_weight,
    proc_recv_weight,
    proc_bias,
    proc_out_weight,
    proc_gain,
    dec_send_weight,
    dec_recv_weight,
    dec_bias,
    dec_out_weight,
    dec_gain,
    enc_src,
    enc_count,
    proc_nbr,
    dec_src,
):
    owners = lax.axis_size("grid")
    my_index = lax.axis_index("grid")
    columns = mesh_state.shape[1]
    grid_rows = grid_feat.shape[0]
    mesh_rows = mesh_state.shape[0]
    grid_count = grid_rows // BLK
    mesh_count = mesh_rows // BLK
    grid_pre = jnp.dot(grid_feat, embed_weight, preferred_element_type=jnp.float32)
    row_sum, row_squares = lax.psum(
        (jnp.sum(grid_pre, axis=1), jnp.sum(grid_pre * grid_pre, axis=1)), ("mesh", "sub")
    )
    grid_state = normalize(grid_pre, row_sum, row_squares, embed_gain).astype(jnp.bfloat16)
    enc_send_sum, dec_recv = fold_projection(
        (enc_send_weight, dec_recv_weight),
        lax.all_gather(grid_state, ("mesh", "sub"), axis=1, tiled=True),
    )
    enc_send = enc_send_sum.astype(jnp.bfloat16).reshape(grid_count, BLK, columns)
    (enc_recv,) = fold_projection(
        (enc_recv_weight,), lax.all_gather(mesh_state, ("mesh", "sub"), axis=1, tiled=True)
    )
    fanout = enc_src.shape[1]
    enc_rows = lax.dynamic_slice_in_dim(enc_src, my_index * mesh_count, mesh_count, 0)
    enc_counts = lax.dynamic_slice_in_dim(enc_count, my_index * mesh_count, mesh_count, 0)
    fan_ids = jnp.arange(fanout, dtype=jnp.int32)
    enc_mask = fan_ids[None, :] < enc_counts[:, None]
    enc_table = block_table(enc_rows.reshape(-1), enc_mask.reshape(-1), owners * grid_count)
    enc_picked = fold_select(enc_table, lax.all_gather(enc_send, "grid", axis=0, tiled=True))
    enc_hidden = edge_sum(
        enc_picked,
        enc_recv.reshape(mesh_count, BLK, columns),
        enc_bias,
        enc_mask.astype(jnp.float32),
    )
    (enc_out,) = fold_projection(
        (enc_out_weight,), lax.all_gather(enc_hidden, ("mesh", "sub"), axis=1, tiled=True)
    )
    mesh_mid = (mesh_state.astype(jnp.float32) + norm_columns(enc_out, enc_gain)).astype(
        jnp.bfloat16
    )
    proc_send_sum, proc_recv = fold_projection(
        (proc_send_weight, proc_recv_weight),
        lax.all_gather(mesh_mid, ("mesh", "sub"), axis=1, tiled=True),
    )
    proc_send = proc_send_sum.astype(jnp.bfloat16).reshape(mesh_count, BLK, columns)
    window = extended(proc_send, (("grid", 0),), mesh_count)
    nbr_rows = lax.dynamic_slice_in_dim(proc_nbr, my_index * mesh_count, mesh_count, 0)
    nbr_owner = nbr_rows // mesh_count
    relative = (nbr_owner - my_index + 1 + owners) % owners
    slot_place = relative * mesh_count + (nbr_rows - nbr_owner * mesh_count)
    nbr_table = (
        slot_place.reshape(-1)[:, None] == jnp.arange(3 * mesh_count, dtype=jnp.int32)[None, :]
    ).astype(jnp.bfloat16)
    proc_picked = jnp.dot(
        nbr_table, window.reshape(3 * mesh_count, -1), preferred_element_type=jnp.float32
    )
    proc_hidden = edge_sum(
        proc_picked,
        proc_recv.reshape(mesh_count, BLK, columns),
        proc_bias,
        jnp.ones(nbr_rows.shape, jnp.float32),
    )
    (proc_out,) = fold_projection(
        (proc_out_weight,), lax.all_gather(proc_hidden, ("mesh", "sub"), axis=1, tiled=True)
    )
    mesh_out = (mesh_mid.astype(jnp.float32) + norm_columns(proc_out, proc_gain)).astype(
        jnp.bfloat16
    )
    (dec_send_sum,) = fold_projection(
        (dec_send_weight,), lax.all_gather(mesh_out, ("mesh", "sub"), axis=1, tiled=True)
    )
    dec_send = dec_send_sum.astype(jnp.bfloat16).reshape(mesh_count, BLK, columns)
    dec_rows = lax.dynamic_slice_in_dim(dec_src, my_index * grid_count, grid_count, 0)
    dec_mask = jnp.ones(dec_rows.shape, jnp.bool_)
    dec_table = block_table(dec_rows.reshape(-1), dec_mask.reshape(-1), owners * mesh_count)
    dec_picked = fold_select(dec_table, lax.all_gather(dec_send, "grid", axis=0, tiled=True))
    dec_hidden = edge_sum(
        dec_picked,
        dec_recv.reshape(grid_count, BLK, columns),
        dec_bias,
        dec_mask.astype(jnp.float32),
    )
    (dec_out,) = fold_projection(
        (dec_out_weight,), lax.all_gather(dec_hidden, ("mesh", "sub"), axis=1, tiled=True)
    )
    grid_out = (grid_state.astype(jnp.float32) + norm_columns(dec_out, dec_gain)).astype(
        jnp.bfloat16
    )
    return (grid_out, mesh_out)


def solution(mesh):
    return jax.shard_map(
        on_device,
        mesh=mesh,
        in_specs=(
            P(("groups", "grid"), None),
            P(("groups", "grid"), ("mesh", "sub")),
            P(None, ("mesh", "sub")),
            P(("mesh", "sub")),
            P(None, ("mesh", "sub")),
            P(None, ("mesh", "sub")),
            P(("mesh", "sub")),
            P(None, ("mesh", "sub")),
            P(("mesh", "sub")),
            P(None, ("mesh", "sub")),
            P(None, ("mesh", "sub")),
            P(("mesh", "sub")),
            P(None, ("mesh", "sub")),
            P(("mesh", "sub")),
            P(None, ("mesh", "sub")),
            P(None, ("mesh", "sub")),
            P(("mesh", "sub")),
            P(None, ("mesh", "sub")),
            P(("mesh", "sub")),
            P("groups", None),
            P("groups"),
            P("groups", None),
            P("groups", None),
        ),
        out_specs=(P(("groups", "grid"), ("mesh", "sub")), P(("groups", "grid"), ("mesh", "sub"))),
        check_vma=False,
    )
```

profile of v0, /device:TPU:0, one launch (start us, length us, event | category | flops | bytes accessed | tf_op | source)
XLA Modules:
  0.0 222.5 jit_solution(3539481909127929641)
XLA Ops:
  7.2 0.0 copy-start
  7.2 0.0 all-gather.4.cloned.1.call-start
  7.2 1.0 copy-done
  8.2 1.3 fusion.22
  9.5 8.5 %all-reduce.3 = (f32[1024]{0:T(1024)S(1)}, f32[1024]{0:T(1024)S(1)}) all-reduce(f32[1024]{0:T(1024)S(1)} %get-tuple-element.13, f32[1024]{0:T(1024)S(1)} %get-tuple-element.12), channel_id=1, replica_groups=mesh['groups'=2,'grid'=4,'mesh'=2,'sub'=2] {'mesh','sub'}, use_global_device_ids=true, to_apply=%region_3.0 | all-reduce | flops 2048 | bytes 16384 | tf_op jit(solution)/shard_map/psum | solution.py:101
  18.0 1.6 multiply_convert_fusion
  19.6 0.0 all-gather.4.cloned.1.call-update
  19.7 0.0 copy-start.18
  19.7 0.0 copy-start.6
  19.7 0.0 copy-start.8
  19.7 0.0 all-gather.6.cloned.1.call-start
  19.8 22.9 %all-gather.4.cloned.1.call-done = bf16[1024,1024]{0,1:T(8,128)(2,1)} async-done(((bf16[1024,256]{0,1:T(8,128)(2,1)}), bf16[1024,1024]{0,1:T(8,128)(2,1)}) %all-gather.4.cloned.1.call-update) | async-done | bytes 2097168 | tf_op jit(solution)/shard_map/all_gather | solution.py:107
  42.7 3.2 %convolution_convert_fusion = bf16[1024,256]{1,0:T(8,128)(2,1)} fusion(bf16[1024,1024]{0,1:T(8,128)(2,1)} %all-gather.4.cloned.1.call-done, bf16[1024,256]{1,0:T(8,128)(2,1)S(1)} %copy-done.13), kind=kOutput, calls=%fused_computation.5 | convolution fusion | flops 537133056 | bytes 3145728 | tf_op jit(solution)/shard_map/dot_general | solution.py:45
  45.9 0.0 all-gather.6.cloned.1.call-update
  45.9 0.0 all-gather.8.cloned.1.call-start
  46.0 0.1 dynamic_slice.14
  46.0 0.1 fusion.18
  46.1 0.1 copy.48
  46.2 0.2 copy.46
  46.4 0.9 constant_dynamic-slice_fusion
  47.3 0.1 constant_dynamic-slice_fusion.1
  47.3 0.1 iota_compare_fusion.3
  47.4 8.6 %all_gather.29 = bf16[384,1024]{1,0:T(8,128)(2,1)S(1)} all-gather(bf16[384,256]{1,0:T(8,128)(2,1)S(1)} %copy-done.2), channel_id=1, replica_groups=mesh['groups'=2,'grid'=4,'mesh'=2,'sub'=2] {'mesh','sub'}, dimensions={1}, use_global_device_ids=true | all-gather | bytes 983040 | tf_op jit(solution)/shard_map/all_gather | solution.py:111
  56.0 0.4 fusion.25
  56.4 1.8 fusion.27
  58.2 0.0 copy-start.15
  58.2 0.6 copy.51
  58.8 32.9 %all-gather.6.cloned.1.call-done = bf16[32,128,256]{2,1,0:T(8,128)(2,1)} async-done(((bf16[8,128,256]{2,1,0:T(8,128)(2,1)}), bf16[32,128,256]{2,1,0:T(8,128)(2,1)}) %all-gather.6.cloned.1.call-update) | async-done | bytes 2097168 | tf_op jit(solution)/shard_map/all_gather | solution.py:119
  91.7 5.6 %multiply_reduce_fusion = bf16[3,128,256]{2,1,0:T(8,128)(2,1)S(1)} fusion(f32[3,16]{1,0:T(4,128)S(1)} %get-tuple-element.35, f32[256]{0:T(256)S(1)} %copy-done.15, f32[3,128,256]{2,1,0:T(8,128)S(1)} %bitcast.97, s32[3,16]{1,0:T(4,128)S(1)} %constant_dynamic-slice_fusion, pred[3,16]{1,0:T(4,128)(4,1)S(1)} %get-tuple-element.34, ...), kind=kOutput, calls=%fused_computation | convolution fusion | flops 113150976 | bytes 2688432 | tf_op jit(solution)/shard_map/dot_general | solution.py:51
  97.4 8.6 %all_gather.30 = bf16[384,1024]{1,0:T(8,128)(2,1)S(1)} all-gather(bf16[384,256]{1,0:T(8,128)(2,1)S(1)} %bitcast.101), channel_id=1, replica_groups=mesh['groups'=2,'grid'=4,'mesh'=2,'sub'=2] {'mesh','sub'}, dimensions={1}, use_global_device_ids=true | all-gather | bytes 983040 | tf_op jit(solution)/shard_map/all_gather | solution.py:127
  106.0 0.5 fusion.24
  106.5 6.5 %all-reduce.2 = (f32[384]{0:T(512)S(1)}, f32[384]{0:T(512)S(1)}) all-reduce(f32[384]{0:T(512)S(1)} %get-tuple-element.17, f32[384]{0:T(512)S(1)} %get-tuple-element.16), channel_id=1, replica_groups=mesh['groups'=2,'grid'=4,'mesh'=2,'sub'=2] {'mesh','sub'}, use_global_device_ids=true, to_apply=%region_8.9 | all-reduce | flops 768 | bytes 6144 | tf_op jit(solution)/shard_map/psum | solution.py:36
  113.0 0.1 add_convert_fusion.2
  113.1 8.2 %all_gather.31 = bf16[384,1024]{0,1:T(8,128)(2,1)S(1)} all-gather(bf16[384,256]{0,1:T(8,128)(2,1)S(1)} %add_convert_fusion.2), channel_id=1, replica_groups=mesh['groups'=2,'grid'=4,'mesh'=2,'sub'=2] {'mesh','sub'}, dimensions={1}, use_global_device_ids=true | all-gather | bytes 983040 | tf_op jit(solution)/shard_map/all_gather | solution.py:134
  121.4 1.7 convolution_convert_fusion.2
  123.1 1.2 collective-permute-start.1
  124.3 0.9 collective-permute-start
  125.2 0.1 concatenate.11
  125.3 1.7 fusion.26
  127.0 3.5 %collective-permute-done.1 = bf16[3,128,256]{2,1,0:T(8,128)(2,1)} collective-permute-done((bf16[3,128,256]{2,1,0:T(8,128)(2,1)S(1)}, bf16[3,128,256]{2,1,0:T(8,128)(2,1)}, u32[]{:S(2)}, u32[]{:S(2)}) %collective-permute-start.1) | collective-permute-done | bytes 196640 | tf_op jit(solution)/shard_map/ppermute | solution.py:22
  130.4 1.1 copy.61
  131.5 3.7 %collective-permute-done = bf16[3,128,256]{2,1,0:T(8,128)(2,1)S(1)} collective-permute-done((bf16[3,128,256]{2,1,0:T(8,128)(2,1)S(1)}, bf16[3,128,256]{2,1,0:T(8,128)(2,1)S(1)}, u32[]{:S(2)}, u32[]{:S(2)}) %collective-permute-start) | collective-permute-done | bytes 196640 | tf_op jit(solution)/shard_map/ppermute | solution.py:20
  135.2 0.2 copy.60
  135.4 0.6 pad_maximum_fusion
  136.0 0.2 copy.62
  136.3 0.4 copy-done.16
  136.7 2.3 %multiply_reduce_fusion.2 = bf16[3,128,256]{2,1,0:T(8,128)(2,1)S(1)} fusion(f32[256]{0:T(256)S(1)} %copy-done.16, f32[3,128,256]{2,1,0:T(8,128)S(1)} %bitcast.105, bf16[128,256,9]{1,0,2:T(8,128)(2,1)S(1)} %slice_bitcast_fusion.1, s32[3,6]{1,0:T(4,128)S(1)} %copy.48), kind=kOutput, calls=%fused_computation.2 | convolution fusion | flops 14647458 | bytes 1180744 | tf_op jit(solution)/shard_map/dot_general | solution.py:145
  139.0 8.0 %all_gather.32 = bf16[384,1024]{1,0:T(8,128)(2,1)S(1)} all-gather(bf16[384,256]{1,0:T(8,128)(2,1)S(1)} %bitcast.102), channel_id=1, replica_groups=mesh['groups'=2,'grid'=4,'mesh'=2,'sub'=2] {'mesh','sub'}, dimensions={1}, use_global_device_ids=true | all-gather | bytes 983040 | tf_op jit(solution)/shard_map/all_gather | solution.py:155
  147.0 0.5 fusion.23
  147.5 6.7 %all-reduce.1 = (f32[384]{0:T(512)S(1)}, f32[384]{0:T(512)S(1)}) all-reduce(f32[384]{0:T(512)S(1)} %get-tuple-element.15, f32[384]{0:T(512)S(1)} %get-tuple-element.14), channel_id=1, replica_groups=mesh['groups'=2,'grid'=4,'mesh'=2,'sub'=2] {'mesh','sub'}, use_global_device_ids=true, to_apply=%region_13.14 | all-reduce | flops 768 | bytes 6144 | tf_op jit(solution)/shard_map/psum | solution.py:36
  154.3 0.1 add_convert_fusion.1
  154.4 8.0 %all_gather.33 = bf16[384,1024]{0,1:T(8,128)(2,1)S(1)} all-gather(bf16[384,256]{0,1:T(8,128)(2,1)S(1)} %add_convert_fusion.1), channel_id=1, replica_groups=mesh['groups'=2,'grid'=4,'mesh'=2,'sub'=2] {'mesh','sub'}, dimensions={1}, use_global_device_ids=true | all-gather | bytes 983040 | tf_op jit(solution)/shard_map/all_gather | solution.py:161
  162.4 1.5 convolution_convert_fusion.1
  163.9 18.0 %all_gather.34 = bf16[12,128,256]{2,1,0:T(8,128)(2,1)S(1)} all-gather(bf16[3,128,256]{2,1,0:T(8,128)(2,1)S(1)} %bitcast.103), channel_id=1, replica_groups=mesh['groups'=2,'grid'=4,'mesh'=2,'sub'=2] {'grid'}, dimensions={0}, use_global_device_ids=true | all-gather | bytes 983040 | tf_op jit(solution)/shard_map/all_gather | solution.py:167
  181.9 0.1 slice_bitcast_fusion
  182.0 1.3 multiply_reduce_fusion.1
  183.2 0.9 copy.52
  184.1 0.0 all-gather.8.cloned.1.call-update
  184.2 0.8 copy.54
  185.0 21.3 %all-gather.8.cloned.1.call-done = bf16[1024,1024]{1,0:T(8,128)(2,1)} async-done(((bf16[1024,256]{1,0:T(8,128)(2,1)}), bf16[1024,1024]{1,0:T(8,128)(2,1)}) %all-gather.8.cloned.1.call-update) | async-done | bytes 2097168 | tf_op jit(solution)/shard_map/all_gather | solution.py:175
  206.3 2.4 %fusion.21 = (f32[1024]{0:T(1024)S(1)}, f32[1024]{0:T(1024)S(1)}, f32[1024,256]{0,1:T(8,128)S(1)}) fusion(bf16[1024,1024]{1,0:T(8,128)(2,1)} %all-gather.8.cloned.1.call-done, bf16[1024,256]{1,0:T(8,128)(2,1)S(1)} %copy-done.14), kind=kOutput, calls=%fused_computation.56 | convolution fusion | flops 537655296 | bytes 3678208 | tf_op jit(solution)/shard_map/dot_general | solution.py:45
  208.6 6.0 %all-reduce = (f32[1024]{0:T(1024)S(1)}, f32[1024]{0:T(1024)S(1)}) all-reduce(f32[1024]{0:T(1024)S(1)} %get-tuple-element.11, f32[1024]{0:T(1024)S(1)} %get-tuple-element.10), channel_id=1, replica_groups=mesh['groups'=2,'grid'=4,'mesh'=2,'sub'=2] {'mesh','sub'}, use_global_device_ids=true, to_apply=%region_18.19 | all-reduce | flops 2048 | bytes 16384 | tf_op jit(solution)/shard_map/psum | solution.py:36
  214.7 0.3 add_convert_fusion
  215.0 1.0 copy.53
  (36 shorter events, 0.2 us)
Async XLA Ops:
  7.2 1.0 copy-start
  7.2 35.5 %copy-start.13 = (bf16[1024,256]{1,0:T(8,128)(2,1)S(1)}, bf16[1024,256]{1,0:T(8,128)(2,1)}, u32[]{:S(2)}) copy-start(bf16[1024,256]{1,0:T(8,128)(2,1)} %param.27) | copy-start | bytes 1572868
  7.2 35.5 %all-gather.4.cloned.1.call-start = ((), (), s32[]{:S(2)}) async-start(), calls=%async_computation | async-start | bytes 2621440 | tf_op jit(solution)/shard_map/all_gather | solution.py:107
  19.7 26.3 %copy-start.18 = (s32[12]{0:T(128)S(1)}, s32[12]{0:T(128)}, u32[]{:S(2)}) copy-start(s32[12]{0:T(128)} %param.43) | copy-start | bytes 148
  19.7 26.4 %copy-start.6 = (s32[12,6]{0,1:T(8,128)S(1)}, s32[12,6]{0,1:T(8,128)}, u32[]{:S(2)}) copy-start(s32[12,6]{0,1:T(8,128)} %param.44) | copy-start | bytes 868
  19.7 26.5 %copy-start.2 = (bf16[384,256]{1,0:T(8,128)(2,1)S(1)}, bf16[384,256]{1,0:T(8,128)(2,1)}, u32[]{:S(2)}) copy-start(bf16[384,256]{1,0:T(8,128)(2,1)} %param.24) | copy-start | bytes 589828
  19.7 27.6 %copy-start.8 = (s32[32,3]{0,1:T(4,128)S(1)}, s32[32,3]{0,1:T(4,128)}, u32[]{:S(2)}) copy-start(s32[32,3]{0,1:T(4,128)} %param.45) | copy-start | bytes 1156
  19.7 72.0 %all-gather.6.cloned.1.call-start = ((), (), s32[]{:S(2)}) async-start(), calls=%async_computation.1 | async-start | bytes 2621440 | tf_op jit(solution)/shard_map/all_gather | solution.py:119
  45.9 10.1 %copy-start.3 = (bf16[1024,256]{1,0:T(8,128)(2,1)S(1)}, bf16[1024,256]{1,0:T(8,128)(2,1)}, u32[]{:S(2)}) copy-start(bf16[1024,256]{1,0:T(8,128)(2,1)} %param.28) | copy-start | bytes 1572868
  45.9 160.4 %all-gather.8.cloned.1.call-start = ((), (), s32[]{:S(2)}) async-start(), calls=%async_computation.2 | async-start | bytes 2621440 | tf_op jit(solution)/shard_map/all_gather | solution.py:175
  46.4 10.0 %copy-start.12 = (bf16[1024,1024]{0,1:T(8,128)(2,1)S(1)}, bf16[1024,1024]{0,1:T(8,128)(2,1)}, u32[]{:S(2)}) copy-start(bf16[1024,1024]{0,1:T(8,128)(2,1)} %all-gather.4.cloned.1.call-done) | copy-start | bytes 6291460
  58.2 33.6 %copy-start.15 = (f32[256]{0:T(256)S(1)}, f32[256]{0:T(256)}, u32[]{:S(2)}) copy-start(f32[256]{0:T(256)} %param.29) | copy-start | bytes 3076
  91.7 14.2 %copy-start.4 = (bf16[1024,256]{1,0:T(8,128)(2,1)S(1)}, bf16[1024,256]{1,0:T(8,128)(2,1)}, u32[]{:S(2)}) copy-start(bf16[1024,256]{1,0:T(8,128)(2,1)} %param.30) | copy-start | bytes 1572868
  97.4 15.6 %copy-start.9 = (f32[256]{0:T(256)S(1)}, f32[256]{0:T(256)}, u32[]{:S(2)}) copy-start(f32[256]{0:T(256)} %param.31) | copy-start | bytes 3076
  121.4 3.0 %copy-start.1 = (bf16[384,1024]{0,1:T(8,128)(2,1)}, bf16[384,1024]{0,1:T(8,128)(2,1)S(1)}, u32[]{:S(2)}) copy-start(bf16[384,1024]{0,1:T(8,128)(2,1)S(1)} %all_gather.31) | copy-start | bytes 2359300
  123.1 7.3 %collective-permute-start.1 = (bf16[3,128,256]{2,1,0:T(8,128)(2,1)S(1)}, bf16[3,128,256]{2,1,0:T(8,128)(2,1)}, u32[]{:S(2)}, u32[]{:S(2)}) collective-permute-start(bf16[3,128,256]{2,1,0:T(8,128)(2,1)S(1)} %bitcast.98), channel_id=1, source_target_pairs={{4,0},{8,4},{12,8},{0,12},{5,1},{9,5},{13,9},{1,13},{6,2},{10,6},{... | collective-permute-start | bytes 589832 | tf_op jit(solution)/shard_map/ppermute | solution.py:22
  124.3 10.9 %collective-permute-start = (bf16[3,128,256]{2,1,0:T(8,128)(2,1)S(1)}, bf16[3,128,256]{2,1,0:T(8,128)(2,1)S(1)}, u32[]{:S(2)}, u32[]{:S(2)}) collective-permute-start(bf16[3,128,256]{2,1,0:T(8,128)(2,1)S(1)} %bitcast.99), channel_id=1, source_target_pairs={{0,4},{4,8},{8,12},{12,0},{1,5},{5,9},{9,13},{13,1},{2,6},{6,10},{... | collective-permute-start | bytes 589832 | tf_op jit(solution)/shard_map/ppermute | solution.py:20
  136.0 0.7 copy-start.16
  136.7 10.3 %copy-start.5 = (bf16[1024,256]{1,0:T(8,128)(2,1)S(1)}, bf16[1024,256]{1,0:T(8,128)(2,1)}, u32[]{:S(2)}) copy-start(bf16[1024,256]{1,0:T(8,128)(2,1)} %param.35) | copy-start | bytes 1572868
  139.0 15.3 %copy-start.10 = (f32[256]{0:T(256)S(1)}, f32[256]{0:T(256)}, u32[]{:S(2)}) copy-start(f32[256]{0:T(256)} %param.36) | copy-start | bytes 3076
  162.4 19.5 %copy-start.17 = (f32[256]{0:T(256)S(1)}, f32[256]{0:T(256)}, u32[]{:S(2)}) copy-start(f32[256]{0:T(256)} %param.39) | copy-start | bytes 3076
  181.9 24.3 %copy-start.14 = (bf16[1024,256]{1,0:T(8,128)(2,1)S(1)}, bf16[1024,256]{1,0:T(8,128)(2,1)}, u32[]{:S(2)}) copy-start(bf16[1024,256]{1,0:T(8,128)(2,1)} %param.40) | copy-start | bytes 1572868
  184.2 30.5 %copy-start.7 = (f32[256]{0:T(256)S(1)}, f32[256]{0:T(256)}, u32[]{:S(2)}) copy-start(f32[256]{0:T(256)} %param.26) | copy-start | bytes 3076
  184.2 30.5 %copy-start.11 = (f32[256]{0:T(256)S(1)}, f32[256]{0:T(256)}, u32[]{:S(2)}) copy-start(f32[256]{0:T(256)} %param.41) | copy-start | bytes 3076
Sparse Core Ops, SparseCore 0:
  19.8 22.8 all-gather.3
  46.0 45.6 all-gather.5
  184.3 21.9 all-gather.7
where the time goes:
time: 223 us
  blocking collectives  87.2 us (39%)
  waiting for transfers between devices  84.3 us (38%)
  matrix products  24.1 us (11%)
  between operations  14.1 us (6%)
  local copies, waits for them, and re-layouts  7.73 us (3%)
  other arithmetic  2.97 us (1%)
    all_gather x1, waiting for transfers between devices, on_device(): lax.all_gather(enc_send, 'grid', axis=0, tiled=True)  32.9 us
    all_gather x1, waiting for transfers between devices, on_device(): lax.all_gather(grid_state, ('mesh', 'sub'), axis=1, tiled=True)  22.9 us
    all_gather x1, waiting for transfers between devices, on_device(): lax.all_gather(dec_hidden, ('mesh', 'sub'), axis=1, tiled=True)  21.3 us
    psum x3, blocking collectives, norm_columns(): lax.psum((jnp.sum(partial_value, axis=1), jnp.sum(partial_value * partial...  19.3 us
    all_gather x1, blocking collectives, on_device(): lax.all_gather(dec_send, 'grid', axis=0, tiled=True)  18 us
    dot_general x9, matrix products, fold_projection(): jnp.dot(shard_piece, weight, preferred_element_type=jnp.float32)  13.6 us
    all_gather x1, blocking collectives, on_device(): lax.all_gather(enc_hidden, ('mesh', 'sub'), axis=1, tiled=True)  8.57 us
    all_gather x1, blocking collectives, on_device(): lax.all_gather(mesh_state, ('mesh', 'sub'), axis=1, tiled=True)  8.57 us
  transfers between devices with their start and end apart: 5, of which 5 were waited for; matrix products, arithmetic and copies ran while one was open for 4% of the time, Pallas kernels for 0%

commit v1 on v0

v1 whole, which is shorter than its diff:
```python
import functools

import jax
import jax.numpy as jnp
from jax import lax
from jax.experimental import pallas as pl
from jax.experimental.pallas import tpu as pltpu
from jax.sharding import PartitionSpec as P

BLK = 128
EPSILON = 1e-05
MESH_ID = pl.DeviceIdType.MESH
F32 = jnp.float32
BF16 = jnp.bfloat16
SUBROWS = 32


class Drain:
    def __init__(self):
        self.sent = []

    def send(self, src, dst, send_sem, recv_sem, device):
        copy = pltpu.make_async_remote_copy(
            src_ref=src, dst_ref=dst, send_sem=send_sem, recv_sem=recv_sem,
            device_id=device, device_id_type=MESH_ID,
        )
        copy.start()
        self.sent.append(copy)

    def arrived(self, dst, send_sem, recv_sem, device):
        pltpu.make_async_remote_copy(
            src_ref=dst, dst_ref=dst, send_sem=send_sem, recv_sem=recv_sem,
            device_id=device, device_id_type=MESH_ID,
        ).wait_recv()

    def finish(self):
        for copy in self.sent:
            copy.wait_send()


class Gather:
    def __init__(self, drain, sizes, place, view, sems, chunks):
        self.drain, self.view = drain, view
        self.xs, self.xr, self.ss, self.sr = sems
        self.mx, self.subs = sizes
        self.m, self.s = place
        self.chunks = chunks

    def shard(self, j, t):
        return lax.rem(self.m + self.mx - j, self.mx) * self.subs + lax.rem(
            self.s + self.subs - t, self.subs
        )

    def xi(self, c, j):
        return c * self.mx + j

    def si(self, c, t, j):
        return (c * self.subs + t) * self.mx + j

    def sib(self, t):
        return {"sub": lax.rem(self.s + t, self.subs)}

    def peer(self, j):
        return {"mesh": lax.rem(self.m + j, self.mx)}

    def issue(self, c, src=None):
        mine = self.view(self.shard(0, 0), c)
        src = mine if src is None else src
        for j in range(1, self.mx):
            i = self.xi(c, j)
            self.drain.send(src, mine, self.xs.at[i], self.xr.at[i], self.peer(j))
        for t in range(1, self.subs):
            i = self.si(c, t, 0)
            self.drain.send(src, mine, self.ss.at[i], self.sr.at[i], self.sib(t))

    def forward(self, c):
        for j in range(1, self.mx):
            i = self.xi(c, j)
            ref = self.view(self.shard(j, 0), c)
            self.drain.arrived(ref, self.xs.at[i], self.xr.at[i], self.peer(j))
            for t in range(1, self.subs):
                k = self.si(c, t, j)
                self.drain.send(ref, ref, self.ss.at[k], self.sr.at[k], self.sib(t))

    def finish(self, c):
        for t in range(1, self.subs):
            for j in range(self.mx):
                k = self.si(c, t, j)
                self.drain.arrived(
                    self.view(self.shard(j, t), c), self.ss.at[k], self.sr.at[k], self.sib(t)
                )


def gather_sems(chunks, mx, subs):
    return [pltpu.SemaphoreType.DMA((chunks * mx,))] * 2 + [
        pltpu.SemaphoreType.DMA((chunks * subs * mx,))
    ] * 2


def edges(target, receiver, bias_free, sources):
    @pl.loop(0, BLK // SUBROWS)
    def _(r):
        rows = pl.ds(pl.multiple_of(r * SUBROWS, SUBROWS), SUBROWS)
        base = receiver(rows)
        total = bias_free(rows)
        for load, weight in sources:
            half = load(rows).astype(F32) + base
            active = half + half * jnp.tanh(half)
            if weight is not None:
                active = active * weight
            total = active if total is None else total + active
        target(rows, total)


def kernel(
    sizes, enc_src, enc_count, proc_nbr, dec_src, params, grid_feat, mesh_state, embed_w,
    es_w, er_w, eo_w, ps_w, pr_w, po_w, ds_w, dr_w, do_w,
    grid_out, mesh_out,
    w_es, w_er, w_eo, w_ps, w_pr, w_po, w_ds, w_dr, w_do,
    we_all, par_all, ms_all, feats, wec, m_enc, m_dec, enc_all, enc_recv,
    hid1, out1, mid_all, win, proc_recv, hid2, out2, mo_all, dsend, dec_recv, gstate,
    hid3, dec_out, stats, g_stage,
    lsem,
    we_xs, we_xr, we_ss, we_sr,
    ms_xs, ms_xr, ms_ss, ms_sr,
    h1_xs, h1_xr, h1_ss, h1_sr,
    o1_xs, o1_xr, o1_ss, o1_sr,
    h2_xs, h2_xr, h2_ss, h2_sr,
    o2_xs, o2_xr, o2_ss, o2_sr,
    h3_xs, h3_xr, h3_ss, h3_sr,
    fz_s, fz_r, fx_s, fx_r, fs_s, fs_r,
    pp_s, pp_r, st_s, st_r, wz_s, wz_r, dz_s, dz_r,
):
    owners, mx, subs = sizes
    nf = mx * subs
    o, m, s = lax.axis_index("grid"), lax.axis_index("mesh"), lax.axis_index("sub")
    f_me = m * subs + s
    mc = mesh_state.shape[0]
    cols = mesh_state.shape[2]
    gr, fin = grid_feat.shape
    gc = gr // BLK
    d_all = nf * cols
    part = gr // nf
    drain = Drain()

    loads = []

    def load(src, dst):
        copy = pltpu.make_async_copy(src, dst, lsem.at[len(loads)])
        copy.start()
        loads.append(copy)
        return copy

    l_we = load(embed_w, we_all.at[f_me])
    l_es = load(es_w, w_es)
    l_dr = load(dr_w, w_dr)
    l_feat = load(grid_feat, feats.at[o])
    l_ms = load(mesh_state, ms_all.at[f_me])
    l_er = load(er_w, w_er)
    l_par = load(params, par_all.at[f_me])
    l_eo, l_ps, l_pr, l_po, l_ds, l_do = (
        load(a, b)
        for a, b in ((eo_w, w_eo), (ps_w, w_ps), (pr_w, w_pr), (po_w, w_po), (ds_w, w_ds), (do_w, w_do))
    )

    feature_peers = []
    for j in range(mx):
        for t in range(subs):
            if j or t:
                feature_peers.append(
                    {"mesh": lax.rem(m + j, mx), "sub": lax.rem(s + t, subs)}
                )
    grid_peers = [{"grid": lax.rem(o + j, owners)} for j in range(1, owners)]
    barrier = pltpu.get_barrier_semaphore()
    for device in feature_peers + grid_peers:
        pl.semaphore_signal(barrier, inc=1, device_id=device, device_id_type=MESH_ID)
    pl.semaphore_wait(barrier, len(feature_peers) + len(grid_peers))

    def gather(view, sems, chunks):
        return Gather(drain, (mx, subs), (m, s), view, sems, chunks)

    g_we = gather(lambda f, c: we_all.at[f], (we_xs, we_xr, we_ss, we_sr), 1)
    g_ms = gather(lambda f, c: ms_all.at[f], (ms_xs, ms_xr, ms_ss, ms_sr), 1)
    block_view = lambda buf: (lambda f, c: buf.at[f, c])
    g_h1 = gather(block_view(hid1), (h1_xs, h1_xr, h1_ss, h1_sr), mc)
    g_o1 = gather(block_view(out1), (o1_xs, o1_xr, o1_ss, o1_sr), mc)
    g_h2 = gather(block_view(hid2), (h2_xs, h2_xr, h2_ss, h2_sr), mc)
    g_o2 = gather(block_view(out2), (o2_xs, o2_xr, o2_ss, o2_sr), mc)
    g_h3 = gather(block_view(hid3), (h3_xs, h3_xr, h3_ss, h3_sr), gc)

    def peer_shard(p):
        j, t = (p + 1) // subs, (p + 1) % subs
        return lax.rem(m + mx - j, mx) * subs + lax.rem(s + subs - t, subs)

    g_we.issue(0, embed_w)
    for p, device in enumerate(feature_peers):
        drain.send(params, par_all.at[f_me], pp_s.at[p], pp_r.at[p], device)
    my_rows = pl.ds(pl.multiple_of(f_me * part, part), part)
    near = sorted(range(1, owners), key=lambda j: (min(j, owners - j), j))
    for j in sorted(range(1, owners), key=lambda j: (-min(j, owners - j), j)):
        drain.send(
            grid_feat.at[my_rows], feats.at[o, my_rows], fz_s.at[j], fz_r.at[j], grid_peers[j - 1]
        )
    g_ms.issue(0, mesh_state)

    def feat_view(j, f):
        rows = pl.ds(pl.multiple_of(f * part, part), part)
        return feats.at[lax.rem(o + owners - j, owners), rows]

    feat_gathers = {}
    for j in range(1, owners):
        g = gather(lambda f, c, j=j: feat_view(j, f), (fx_s, fx_r, fs_s, fs_r), owners)
        feat_gathers[j] = g

    g_we.forward(0)
    l_we.wait()
    g_we.finish(0)
    l_par.wait()
    for p, device in enumerate(feature_peers):
        drain.arrived(par_all.at[peer_shard(p)], pp_s.at[p], pp_r.at[p], device)
    l_es.wait()
    l_dr.wait()

    row_sum = None
    for f in range(nf):
        one = jnp.sum(we_all[f].astype(F32), axis=1, keepdims=True)
        row_sum = one if row_sum is None else row_sum + one
    row_mean = row_sum / d_all
    enc_map = dec_map = None
    for f in range(nf):
        centred = we_all[f].astype(F32) - row_mean
        wec[f] = centred.astype(BF16)
        gained = (centred * par_all[f, 0:1, :]).astype(BF16)
        a = jnp.dot(gained, w_es[f * cols : (f + 1) * cols, :], preferred_element_type=F32)
        b = jnp.dot(gained, w_dr[f * cols : (f + 1) * cols, :], preferred_element_type=F32)
        enc_map = a if enc_map is None else enc_map + a
        dec_map = b if dec_map is None else dec_map + b
    m_enc[...] = (0.5 * enc_map).astype(BF16)
    m_dec[...] = (0.5 * dec_map).astype(BF16)

    pair = 2 if gc % 2 == 0 else 1

    def project(owner, own):
        @pl.loop(0, gc // pair)
        def _(i):
            rows = pl.ds(pl.multiple_of(i * (pair * BLK), pair * BLK), pair * BLK)
            x = feats[owner, rows, :]
            squares = None
            for f in range(nf):
                v = jnp.dot(x, wec[f], preferred_element_type=F32)
                one = jnp.sum(v * v, axis=1, keepdims=True)
                squares = one if squares is None else squares + one
            scale = lax.rsqrt(squares / d_all + EPSILON)
            sent = jnp.dot(x, m_enc[...], preferred_element_type=F32) * scale
            blocks = pl.ds(owner * gc + i * pair, pair)
            enc_all[blocks] = sent.reshape(pair, BLK, cols)
            if own:
                got = jnp.dot(x, m_dec[...], preferred_element_type=F32) * scale
                got = got + 0.5 * params[6:7, :]
                dec_recv[pl.ds(i * pair, pair)] = got.reshape(pair, BLK, cols)
                state = jnp.dot(x, wec[f_me], preferred_element_type=F32) * scale
                state = (state * params[0:1, :]).astype(BF16)
                gstate[pl.ds(i * pair, pair)] = state.reshape(pair, BLK, cols)

    l_feat.wait()
    for j in near:
        g = feat_gathers[j]
        drain.arrived(feat_view(j, f_me), fz_s.at[j], fz_r.at[j], grid_peers[j - 1])
        g.issue(j)
    project(o, True)
    for j in near:
        feat_gathers[j].forward(j)
    g_ms.forward(0)
    l_ms.wait()
    g_ms.finish(0)
    l_er.wait()

    def product(buf, b, weight):
        total = None
        for f in range(nf):
            one = jnp.dot(buf[f, b], weight[f * cols : (f + 1) * cols, :], preferred_element_type=F32)
            total = one if total is None else total + one
        return total

    for b in range(mc):
        enc_recv[b] = 0.5 * (product(ms_all, b, w_er) + params[4:5, :])
    for j in near:
        feat_gathers[j].finish(j)
        project(lax.rem(o + owners - j, owners), False)

    fan = enc_src.shape[1]
    for b in range(mc):
        row = o * mc + b
        count = enc_count[row, 0]
        sources = []
        for k in range(fan):
            idx = jnp.clip(enc_src[row, k], 0, owners * gc - 1)
            weight = jnp.where(k < count, 1.0, 0.0).astype(F32)
            sources.append((lambda rows, idx=idx: enc_all[idx, rows, :], weight))

        def put(rows, value, b=b):
            hid1[f_me, b, rows, :] = value.astype(BF16)

        edges(put, lambda rows, b=b: enc_recv[b, rows, :], lambda rows: None, sources)
        g_h1.issue(b)

    def node_layer(g_h, hid, weight, g_o, out):
        for b in range(mc):
            g_h.forward(b)
        for b in range(mc):
            g_h.finish(b)
            out[f_me, b] = product(hid, b, weight).astype(BF16)
            g_o.issue(b)
        for b in range(mc):
            g_o.forward(b)

    def norm_rows(out, old, new, b, gain_row):
        @pl.loop(0, BLK // SUBROWS)
        def _(r):
            rows = pl.ds(pl.multiple_of(r * SUBROWS, SUBROWS), SUBROWS)
            total = None
            for f in range(nf):
                one = jnp.sum(out[f, b, rows, :].astype(F32), axis=1, keepdims=True)
                total = one if total is None else total + one
            mean = total / d_all
            squares = None
            for f in range(nf):
                c = out[f, b, rows, :].astype(F32) - mean
                one = jnp.sum(c * c, axis=1, keepdims=True)
                squares = one if squares is None else squares + one
            scale = lax.rsqrt(squares / d_all + EPSILON)
            for f in range(nf):
                c = out[f, b, rows, :].astype(F32) - mean
                value = c * scale * par_all[f, gain_row : gain_row + 1, :]
                new[f, b, rows, :] = (old[f, b, rows, :].astype(F32) + value).astype(BF16)

    l_eo.wait()
    node_layer(g_h1, hid1, w_eo, g_o1, out1)
    l_ps.wait()
    l_pr.wait()
    left, right = {"grid": lax.rem(o + owners - 1, owners)}, {"grid": lax.rem(o + 1, owners)}
    for b in range(mc):
        g_o1.finish(b)
        norm_rows(out1, ms_all, mid_all, b, 1)
        win[1, b] = (0.5 * product(mid_all, b, w_ps)).astype(BF16)
        drain.send(win.at[1, b], win.at[2, b], wz_s.at[2 * b], wz_r.at[2 * b], left)
        drain.send(win.at[1, b], win.at[0, b], wz_s.at[2 * b + 1], wz_r.at[2 * b + 1], right)
    for b in range(mc):
        proc_recv[b] = 0.5 * (product(mid_all, b, w_pr) + params[5:6, :])
    for b in range(mc):
        drain.arrived(win.at[2, b], wz_s.at[2 * b], wz_r.at[2 * b], left)
        drain.arrived(win.at[0, b], wz_s.at[2 * b + 1], wz_r.at[2 * b + 1], right)
    fan = proc_nbr.shape[1]
    for b in range(mc):
        row = o * mc + b
        sources = []
        for q in range(fan):
            side = q * 3 // fan
            home = lax.rem(o + side - 1 + owners, owners)
            idx = jnp.clip(proc_nbr[row, q] - home * mc, 0, mc - 1)
            sources.append((lambda rows, idx=idx, side=side: win[side, idx, rows, :], None))

        def put(rows, value, b=b):
            hid2[f_me, b, rows, :] = value.astype(BF16)

        edges(put, lambda rows, b=b: proc_recv[b, rows, :], lambda rows: None, sources)
        g_h2.issue(b)
    l_po.wait()
    node_layer(g_h2, hid2, w_po, g_o2, out2)
    l_ds.wait()
    for b in range(mc):
        g_o2.finish(b)
        norm_rows(out2, mid_all, mo_all, b, 2)
        dsend[o * mc + b] = (0.5 * product(mo_all, b, w_ds)).astype(BF16)
        for j in range(1, owners):
            i = b * owners + j
            ref = dsend.at[o * mc + b]
            drain.send(ref, ref, dz_s.at[i], dz_r.at[i], grid_peers[j - 1])
    l_out = load(mo_all.at[f_me], mesh_out)
    for b in range(mc):
        for j in near:
            i = b * owners + j
            ref = dsend.at[lax.rem(o + owners - j, owners) * mc + b]
            drain.arrived(ref, dz_s.at[i], dz_r.at[i], grid_peers[j - 1])

    fan = dec_src.shape[1]
    for g in range(gc):
        sources = []
        for e in range(fan):
            idx = jnp.clip(dec_src[o * gc + g, e], 0, owners * mc - 1)
            sources.append((lambda rows, idx=idx: dsend[idx, rows, :], None))

        def put(rows, value, g=g):
            hid3[f_me, g, rows, :] = value.astype(BF16)

        edges(put, lambda rows, g=g: dec_recv[g, rows, :], lambda rows: None, sources)
        g_h3.issue(g)

    l_do.wait()
    eye = lax.broadcasted_iota(jnp.int32, (BLK, BLK), 0) == lax.broadcasted_iota(
        jnp.int32, (BLK, BLK), 1
    )

    top = lax.broadcasted_iota(jnp.int32, (8, BLK), 0) == 0

    def to_row(column):
        return jnp.sum(jnp.where(eye, column, 0.0), axis=0, keepdims=True)

    def to_column(row):
        return jnp.sum(jnp.where(eye, row, 0.0), axis=1, keepdims=True)

    def decode(g):
        g_h3.finish(g)
        value = product(hid3, g, w_do)
        dec_out[g] = value
        sums = to_row(jnp.sum(value, axis=1, keepdims=True))
        squares = to_row(jnp.sum(value * value, axis=1, keepdims=True))
        stats[f_me, g] = jnp.where(top, sums, squares)
        for p, device in enumerate(feature_peers):
            i = g * nf + p
            drain.send(stats.at[f_me, g], stats.at[f_me, g], st_s.at[i], st_r.at[i], device)

    outs = []

    def complete(g):
        for p, device in enumerate(feature_peers):
            i = g * nf + p
            drain.arrived(stats.at[peer_shard(p), g], st_s.at[i], st_r.at[i], device)
        total, squares = stats[0, g, 0:1, :], stats[0, g, 1:2, :]
        for f in range(1, nf):
            total = total + stats[f, g, 0:1, :]
            squares = squares + stats[f, g, 1:2, :]
        mean = total / d_all
        scale = lax.rsqrt(squares / d_all - mean * mean + EPSILON)
        value = (dec_out[g] - to_column(mean)) * to_column(scale) * params[3:4, :]
        g_stage[g] = (gstate[g].astype(F32) + value).astype(BF16)
        outs.append(load(g_stage.at[g], grid_out.at[g]))

    for g in range(gc):
        g_h3.forward(g)
        if g >= 1:
            decode(g - 1)
        if g >= 3:
            complete(g - 3)
    decode(gc - 1)
    for g in range(max(gc - 3, 0), gc):
        complete(g)
    l_out.wait()
    for copy in outs:
        copy.wait()
    drain.finish()


def on_device(
    grid_feat, mesh_state, embed_weight, embed_gain, enc_send_weight, enc_recv_weight, enc_bias,
    enc_out_weight, enc_gain, proc_send_weight, proc_recv_weight, proc_bias, proc_out_weight,
    proc_gain, dec_send_weight, dec_recv_weight, dec_bias, dec_out_weight, dec_gain,
    enc_src, enc_count, proc_nbr, dec_src,
):
    owners, mx, subs = (lax.axis_size(a) for a in ("grid", "mesh", "sub"))
    nf = mx * subs
    mr, cols = mesh_state.shape
    gr, fin = grid_feat.shape
    mc, gc = mr // BLK, gr // BLK
    depth = enc_send_weight.shape[0]
    params = jnp.stack(
        [embed_gain, enc_gain, proc_gain, dec_gain, enc_bias, proc_bias, dec_bias, dec_bias]
    )
    smem = pl.BlockSpec(memory_space=pltpu.SMEM)
    vmem = pl.BlockSpec(memory_space=pltpu.VMEM)
    hbm = pl.BlockSpec(memory_space=pl.ANY)
    dma = pltpu.SemaphoreType.DMA
    scratch = [pltpu.VMEM((depth, cols), BF16)] * 9
    scratch += [
        pltpu.VMEM((nf, fin, cols), BF16),
        pltpu.VMEM((nf, 8, cols), F32),
        pltpu.VMEM((nf, mc, BLK, cols), BF16),
        pltpu.VMEM((owners, gr, fin), BF16),
        pltpu.VMEM((nf, fin, cols), BF16),
        pltpu.VMEM((fin, cols), BF16),
        pltpu.VMEM((fin, cols), BF16),
        pltpu.VMEM((owners * gc, BLK, cols), F32),
        pltpu.VMEM((mc, BLK, cols), F32),
        pltpu.VMEM((nf, mc, BLK, cols), BF16),
        pltpu.VMEM((nf, mc, BLK, cols), BF16),
        pltpu.VMEM((nf, mc, BLK, cols), BF16),
        pltpu.VMEM((3, mc, BLK, cols), BF16),
        pltpu.VMEM((mc, BLK, cols), F32),
        pltpu.VMEM((nf, mc, BLK, cols), BF16),
        pltpu.VMEM((nf, mc, BLK, cols), BF16),
        pltpu.VMEM((nf, mc, BLK, cols), BF16),
        pltpu.VMEM((owners * mc, BLK, cols), BF16),
        pltpu.VMEM((gc, BLK, cols), F32),
        pltpu.VMEM((gc, BLK, cols), BF16),
        pltpu.VMEM((nf, gc, BLK, cols), BF16),
        pltpu.VMEM((gc, BLK, cols), F32),
        pltpu.VMEM((nf, gc, 8, BLK), F32),
        pltpu.VMEM((gc, BLK, cols), BF16),
    ]
    scratch += [dma((14 + gc,))]
    for chunks in (1, 1, mc, mc, mc, mc, gc):
        scratch += gather_sems(chunks, mx, subs)
    scratch += [dma((owners,))] * 2
    scratch += [dma((owners * mx,))] * 2 + [dma((owners * subs * mx,))] * 2
    scratch += [dma((nf,))] * 2 + [dma((gc * nf,))] * 2
    scratch += [dma((2 * mc,))] * 2 + [dma((mc * owners,))] * 2
    grid_out, mesh_out = pl.pallas_call(
        functools.partial(kernel, (owners, mx, subs)),
        out_shape=(
            jax.ShapeDtypeStruct((gc, BLK, cols), BF16),
            jax.ShapeDtypeStruct((mc, BLK, cols), BF16),
        ),
        in_specs=[smem] * 4 + [vmem] + [hbm] * 12,
        out_specs=(hbm, hbm),
        scratch_shapes=scratch,
        compiler_params=pltpu.CompilerParams(
            collective_id=0, has_side_effects=True, vmem_limit_bytes=62 * 1024 * 1024
        ),
        name="graph_step",
    )(
        enc_src, enc_count.reshape(-1, 1), proc_nbr, dec_src, params, grid_feat,
        mesh_state.reshape(mc, BLK, cols), embed_weight, enc_send_weight, enc_recv_weight,
        enc_out_weight, proc_send_weight, proc_recv_weight, proc_out_weight, dec_send_weight,
        dec_recv_weight, dec_out_weight,
    )
    return grid_out.reshape(gr, cols), mesh_out.reshape(mr, cols)


def solution(mesh):
    rows = P(("groups", "grid"), None)
    both = P(("groups", "grid"), ("mesh", "sub"))
    weight = P(None, ("mesh", "sub"))
    vector = P(("mesh", "sub"))
    return jax.shard_map(
        on_device,
        mesh=mesh,
        in_specs=(
            rows, both, weight, vector, weight, weight, vector, weight, vector, weight, weight,
            vector, weight, vector, weight, weight, vector, weight, vector,
            P("groups", None), P("groups"), P("groups", None), P("groups", None),
        ),
        out_specs=(both, both),
        check_vma=False,
    )
```

time: 223 us -> 119 us (0.53)
  Pallas kernels: 0 us -> 110 us
  blocking collectives: 87.2 us -> 0 us
  waiting for transfers between devices: 84.3 us -> 0 us
  matrix products: 24.1 us -> 0 us
  between operations: 14.1 us -> 0.71 us
  other arithmetic: 2.97 us -> 0 us
    pallas_call x0 -> x1, Pallas kernels: none -> 110 us  [on_device(): pl.pallas_call(functools.partial(kernel, (owners, mx, subs)), out_shape=(...]
    all_gather x3 -> x0, waiting for transfers between devices: 77.1 us -> none  [the longest x1 32.9 us: on_device(): lax.all_gather(enc_send, 'grid', axis=0, tiled=True)]
    all_gather x6 -> x0, blocking collectives: 59.4 us -> none  [the longest x1 18 us: on_device(): lax.all_gather(dec_send, 'grid', axis=0, tiled=True)]
    psum x4 -> x0, blocking collectives: 27.8 us -> none  [the longest x3 19.3 us: norm_columns(): lax.psum((jnp.sum(partial_value, axis=1), jnp.sum(partial_value * partial...]
    dot_general x13 -> x0, matrix products: 24.1 us -> none  [the longest x9 13.6 us: fold_projection(): jnp.dot(shard_piece, weight, preferred_element_type=jnp.float32)]
    ppermute x2 -> x0, waiting for transfers between devices: 7.12 us -> none  [the longest x1 3.67 us: extended(): lax.ppermute(tail, axis, [(i, (i + 1) % count) for i in range(count)])]
    unnamed x44 -> x26, local copies, waits for them, and re-layouts: 4.94 us -> 4.72 us
  transfers between devices with their start and end apart: 5 -> 0, of which waited for: 5 -> 0; matrix products, arithmetic and copies ran while one was open for 4% -> 0% of each run, Pallas kernels for 0% -> 0%
where the time goes in v1:
time: 119 us; the launch traced here: 117 us
  Pallas kernels  110 us (92%)
  local copies, waits for them, and re-layouts  6.02 us (5%)
    pallas_call x1, Pallas kernels, on_device(): pl.pallas_call(functools.partial(kernel, (owners, mx, subs)), out_shape=(...  110 us
    unnamed x26, local copies, waits for them, and re-layouts  4.72 us

profile of v1, /device:TPU:0, one launch (start us, length us, event | category | flops | bytes accessed | tf_op | source)
XLA Modules:
  0.0 117.2 jit_solution(3505609257287771701)
XLA Ops:
  0.6 0.0 copy-start.8
  0.6 0.0 copy-start.9
  0.7 0.0 copy-start.6
  0.7 0.0 copy-start.7
  0.7 0.0 copy-start.4
  0.7 0.0 copy-start.5
  0.7 0.0 copy-start.2
  0.7 0.6 copy-done.8
  1.3 0.0 copy-done.9
  1.3 0.0 copy-done.6
  1.3 0.0 copy-done.7
  1.4 0.0 copy-done.4
  1.4 0.0 copy-done.5
  1.4 0.0 copy-done.2
  1.4 0.0 copy-start.10
  1.4 0.6 stack.32.params
  2.0 0.0 copy-done.10
  2.1 0.0 copy-start.1
  2.1 0.7 copy.25.enc_count
  2.8 0.0 copy-done.1
  2.8 0.0 copy-start.3
  2.8 0.7 copy.26.proc_nbr
  3.4 0.0 copy-done.3
  3.4 0.7 copy.27.dec_src
  4.1 110.5 %graph_step.1 = (bf16[8,128,256]{2,1,0:T(8,128)(2,1)}, bf16[3,128,256]{2,1,0:T(8,128)(2,1)}) custom-call(s32[12,16]{1,0:T(8,128)} %enc_src.1, s32[12,1]{1,0:T(8,128)} %copy.25.enc_count, s32[12,6]{1,0:T(8,128)} %copy.26.proc_nbr, s32[32,3]{1,0:T(8,128)} %copy.27.dec_src, f32[8,256]{1,0:T(8,128)} %stack.32.params, bf16[1024,256]{1,0:T(8,128)(2,1)} %grid_feat.1, ...), custom_call_target="tpu_custom_call" | custom-call | tf_op jit(solution)/shard_map/graph_step/pallas_call | solution.py:507
  114.6 0.0 copy-start
  114.6 1.9 %copy.30 = bf16[1024,256]{1,0:T(8,128)(2,1)} copy(bf16[1024,256]{1,0:T(8,128)(2,1)} %bitcast.11) | data formatting | bytes 1048576
  116.5 0.0 copy-done
  116.5 0.7 copy.31
Async XLA Ops:
  0.6 0.7 copy-start.8
  0.6 0.7 copy-start.9
  0.7 0.7 copy-start.6
  0.7 0.7 copy-start.7
  0.7 0.7 copy-start.4
  0.7 0.7 copy-start.5
  0.7 0.7 copy-start.2
  1.4 0.7 copy-start.10
  2.1 0.7 copy-start.1
  2.8 0.7 copy-start.3
  114.6 1.9 %copy-start = (bf16[3,128,256]{2,1,0:T(8,128)(2,1)S(1)}, bf16[3,128,256]{2,1,0:T(8,128)(2,1)}, u32[]{:S(2)}) copy-start(bf16[3,128,256]{2,1,0:T(8,128)(2,1)} %get-tuple-element.5) | copy-start | bytes 589828

commit v2 on v1

--- a/solution.py
+++ b/solution.py
@@ -25,7 +25,19 @@
             device_id=device, device_id_type=MESH_ID,
         )
         copy.start()
-        self.sent.append(copy)
+        self.sent.append((None, copy))
+
+    def send_if(self, wanted, src, dst, send_sem, recv_sem, device):
+        copy = pltpu.make_async_remote_copy(
+            src_ref=src, dst_ref=dst, send_sem=send_sem, recv_sem=recv_sem,
+            device_id=device, device_id_type=MESH_ID,
+        )
+
+        @pl.when(wanted)
+        def _():
+            copy.start()
+
+        self.sent.append((wanted, copy))
 
     def arrived(self, dst, send_sem, recv_sem, device):
         pltpu.make_async_remote_copy(
@@ -34,8 +46,14 @@
         ).wait_recv()
 
     def finish(self):
-        for copy in self.sent:
-            copy.wait_send()
+        for wanted, copy in self.sent:
+            if wanted is None:
+                copy.wait_send()
+            else:
+
+                @pl.when(wanted)
+                def _(copy=copy):
+                    copy.wait_send()
 
 
 class Gather:
@@ -89,6 +107,43 @@
                 self.drain.arrived(
                     self.view(self.shard(j, t), c), self.ss.at[k], self.sr.at[k], self.sib(t)
                 )
+
+
+class Line:
+    def __init__(self, drain, owners, o, view, sems):
+        self.drain, self.owners, self.o, self.view = drain, owners, o, view
+        self.ss, self.rs = sems
+
+    def source(self, i):
+        tables = [
+            sorted((x for x in range(self.owners) if x != r), key=lambda x: (abs(r - x), x))
+            for r in range(self.owners)
+        ]
+        found = jnp.int32(tables[0][i])
+        for r in range(1, self.owners):
+            found = jnp.where(self.o == r, jnp.int32(tables[r][i]), found)
+        return found
+
+    def issue(self, c, src=None):
+        mine = self.view(self.o, c)
+        src = mine if src is None else src
+        arrive = self.rs.at[c * self.owners + self.o]
+        base = c * (self.owners + 1)
+        last = self.owners - 1
+        right = {"grid": jnp.minimum(self.o + 1, last)}
+        left = {"grid": jnp.maximum(self.o - 1, 0)}
+        self.drain.send_if(self.o < last, src, mine, self.ss.at[base + self.o], arrive, right)
+        self.drain.send_if(self.o > 0, src, mine, self.ss.at[base + self.owners], arrive, left)
+
+    def receive(self, source, c):
+        ref = self.view(source, c)
+        arrive = self.rs.at[c * self.owners + source]
+        sent = self.ss.at[c * (self.owners + 1) + source]
+        last = self.owners - 1
+        onward = jnp.where(source < self.o, self.o + 1, self.o - 1)
+        device = {"grid": jnp.clip(onward, 0, last)}
+        self.drain.arrived(ref, sent, arrive, device)
+        self.drain.send_if((onward >= 0) & (onward <= last), ref, ref, sent, arrive, device)
 
 
 def gather_sems(chunks, mx, subs):
@@ -113,11 +168,12 @@
 
 
 def kernel(
-    sizes, enc_src, enc_count, proc_nbr, dec_src, params, grid_feat, mesh_state, embed_w,
+    sizes, enc_src, enc_count, proc_nbr, dec_src, e_gain, c_gain, p_gain, d_gain,
+    e_bias, p_bias, d_bias, grid_feat, mesh_state, embed_w,
     es_w, er_w, eo_w, ps_w, pr_w, po_w, ds_w, dr_w, do_w,
     grid_out, mesh_out,
     w_es, w_er, w_eo, w_ps, w_pr, w_po, w_ds, w_dr, w_do,
-    we_all, par_all, ms_all, feats, wec, m_enc, m_dec, enc_all, enc_recv,
+    we_all, gains, local, ms_all, feats, wec, m_enc, m_dec, enc_all, enc_recv,
     hid1, out1, mid_all, win, proc_recv, hid2, out2, mo_all, dsend, dec_recv, gstate,
     hid3, dec_out, stats, g_stage,
     lsem,
@@ -157,7 +213,9 @@
     l_feat = load(grid_feat, feats.at[o])
     l_ms = load(mesh_state, ms_all.at[f_me])
     l_er = load(er_w, w_er)
-    l_par = load(params, par_all.at[f_me])
+    gain_refs = (e_gain, c_gain, p_gain)
+    l_small = [load(ref, gains.at[k, f_me]) for k, ref in enumerate(gain_refs)]
+    l_small += [load(ref, local.at[k]) for k, ref in enumerate((d_gain, e_bias, p_bias, d_bias))]
     l_eo, l_ps, l_pr, l_po, l_ds, l_do = (
         load(a, b)
         for a, b in ((eo_w, w_eo), (ps_w, w_ps), (pr_w, w_pr), (po_w, w_po), (ds_w, w_ds), (do_w, w_do))
@@ -170,7 +228,8 @@
                 feature_peers.append(
                     {"mesh": lax.rem(m + j, mx), "sub": lax.rem(s + t, subs)}
                 )
-    grid_peers = [{"grid": lax.rem(o + j, owners)} for j in range(1, owners)]
+    left, right = {"grid": lax.rem(o + owners - 1, owners)}, {"grid": lax.rem(o + 1, owners)}
+    grid_peers = [left, right]
     barrier = pltpu.get_barrier_semaphore()
     for device in feature_peers + grid_peers:
         pl.semaphore_signal(barrier, inc=1, device_id=device, device_id_type=MESH_ID)
@@ -194,30 +253,28 @@
 
     g_we.issue(0, embed_w)
     for p, device in enumerate(feature_peers):
-        drain.send(params, par_all.at[f_me], pp_s.at[p], pp_r.at[p], device)
-    my_rows = pl.ds(pl.multiple_of(f_me * part, part), part)
-    near = sorted(range(1, owners), key=lambda j: (min(j, owners - j), j))
-    for j in sorted(range(1, owners), key=lambda j: (-min(j, owners - j), j)):
-        drain.send(
-            grid_feat.at[my_rows], feats.at[o, my_rows], fz_s.at[j], fz_r.at[j], grid_peers[j - 1]
-        )
+        for k, ref in enumerate(gain_refs):
+            i = k * nf + p
+            drain.send(ref, gains.at[k, f_me], pp_s.at[i], pp_r.at[i], device)
+
+    def part_rows(f):
+        return pl.ds(pl.multiple_of(f * part, part), part)
+
+    z_feat = Line(drain, owners, o, lambda c, _: feats.at[c, part_rows(f_me)], (fz_s, fz_r))
+    z_feat.issue(0, grid_feat.at[part_rows(f_me)])
     g_ms.issue(0, mesh_state)
-
-    def feat_view(j, f):
-        rows = pl.ds(pl.multiple_of(f * part, part), part)
-        return feats.at[lax.rem(o + owners - j, owners), rows]
-
-    feat_gathers = {}
-    for j in range(1, owners):
-        g = gather(lambda f, c, j=j: feat_view(j, f), (fx_s, fx_r, fs_s, fs_r), owners)
-        feat_gathers[j] = g
+    g_feat = gather(lambda f, c: feats.at[c, part_rows(f)], (fx_s, fx_r, fs_s, fs_r), owners)
+    others = [z_feat.source(i) for i in range(owners - 1)]
 
     g_we.forward(0)
     l_we.wait()
     g_we.finish(0)
-    l_par.wait()
+    for copy in l_small:
+        copy.wait()
     for p, device in enumerate(feature_peers):
-        drain.arrived(par_all.at[peer_shard(p)], pp_s.at[p], pp_r.at[p], device)
+        for k in range(len(gain_refs)):
+            i = k * nf + p
+            drain.arrived(gains.at[k, peer_shard(p)], pp_s.at[i], pp_r.at[i], device)
     l_es.wait()
     l_dr.wait()
 
@@ -230,7 +287,7 @@
     for f in range(nf):
         centred = we_all[f].astype(F32) - row_mean
         wec[f] = centred.astype(BF16)
-        gained = (centred * par_all[f, 0:1, :]).astype(BF16)
+        gained = (centred * gains[0, f]).astype(BF16)
         a = jnp.dot(gained, w_es[f * cols : (f + 1) * cols, :], preferred_element_type=F32)
         b = jnp.dot(gained, w_dr[f * cols : (f + 1) * cols, :], preferred_element_type=F32)
         enc_map = a if enc_map is None else enc_map + a
@@ -256,21 +313,25 @@
             enc_all[blocks] = sent.reshape(pair, BLK, cols)
             if own:
                 got = jnp.dot(x, m_dec[...], preferred_element_type=F32) * scale
-                got = got + 0.5 * params[6:7, :]
+                got = got + 0.5 * local[3]
                 dec_recv[pl.ds(i * pair, pair)] = got.reshape(pair, BLK, cols)
                 state = jnp.dot(x, wec[f_me], preferred_element_type=F32) * scale
-                state = (state * params[0:1, :]).astype(BF16)
+                state = (state * gains[0, f_me]).astype(BF16)
                 gstate[pl.ds(i * pair, pair)] = state.reshape(pair, BLK, cols)
 
     l_feat.wait()
-    for j in near:
-        g = feat_gathers[j]
-        drain.arrived(feat_view(j, f_me), fz_s.at[j], fz_r.at[j], grid_peers[j - 1])
-        g.issue(j)
+
+    def take(source):
+        z_feat.receive(source, 0)
+        g_feat.issue(source)
+
+    for source in others[:-1]:
+        take(source)
     project(o, True)
-    for j in near:
-        feat_gathers[j].forward(j)
+    take(others[-1])
     g_ms.forward(0)
+    for source in others[:-1]:
+        g_feat.forward(source)
     l_ms.wait()
     g_ms.finish(0)
     l_er.wait()
@@ -283,15 +344,17 @@
         return total
 
     for b in range(mc):
-        enc_recv[b] = 0.5 * (product(ms_all, b, w_er) + params[4:5, :])
-    for j in near:
-        feat_gathers[j].finish(j)
-        project(lax.rem(o + owners - j, owners), False)
+        enc_recv[b] = 0.5 * (product(ms_all, b, w_er) + local[1])
+    for i, source in enumerate(others):
+        if i == len(others) - 1:
+            g_feat.forward(source)
+        g_feat.finish(source)
+        project(source, False)
 
     fan = enc_src.shape[1]
     for b in range(mc):
         row = o * mc + b
-        count = enc_count[row, 0]
+        count = enc_count[row]
         sources = []
         for k in range(fan):
             idx = jnp.clip(enc_src[row, k], 0, owners * gc - 1)
@@ -331,14 +394,13 @@
             scale = lax.rsqrt(squares / d_all + EPSILON)
             for f in range(nf):
                 c = out[f, b, rows, :].astype(F32) - mean
-                value = c * scale * par_all[f, gain_row : gain_row + 1, :]
+                value = c * scale * gains[gain_row, f]
                 new[f, b, rows, :] = (old[f, b, rows, :].astype(F32) + value).astype(BF16)
 
     l_eo.wait()
     node_layer(g_h1, hid1, w_eo, g_o1, out1)
     l_ps.wait()
     l_pr.wait()
-    left, right = {"grid": lax.rem(o + owners - 1, owners)}, {"grid": lax.rem(o + 1, owners)}
     for b in range(mc):
         g_o1.finish(b)
         norm_rows(out1, ms_all, mid_all, b, 1)
@@ -346,18 +408,18 @@
         drain.send(win.at[1, b], win.at[2, b], wz_s.at[2 * b], wz_r.at[2 * b], left)
         drain.send(win.at[1, b], win.at[0, b], wz_s.at[2 * b + 1], wz_r.at[2 * b + 1], right)
     for b in range(mc):
-        proc_recv[b] = 0.5 * (product(mid_all, b, w_pr) + params[5:6, :])
+        proc_recv[b] = 0.5 * (product(mid_all, b, w_pr) + local[2])
     for b in range(mc):
         drain.arrived(win.at[2, b], wz_s.at[2 * b], wz_r.at[2 * b], left)
         drain.arrived(win.at[0, b], wz_s.at[2 * b + 1], wz_r.at[2 * b + 1], right)
-    fan = proc_nbr.shape[1]
+    fan = proc_nbr.shape[0]
     for b in range(mc):
         row = o * mc + b
         sources = []
         for q in range(fan):
             side = q * 3 // fan
             home = lax.rem(o + side - 1 + owners, owners)
-            idx = jnp.clip(proc_nbr[row, q] - home * mc, 0, mc - 1)
+            idx = jnp.clip(proc_nbr[q, row] - home * mc, 0, mc - 1)
             sources.append((lambda rows, idx=idx, side=side: win[side, idx, rows, :], None))
 
         def put(rows, value, b=b):
@@ -368,26 +430,22 @@
     l_po.wait()
     node_layer(g_h2, hid2, w_po, g_o2, out2)
     l_ds.wait()
+    z_dec = Line(drain, owners, o, lambda c, b: dsend.at[c * mc + b], (dz_s, dz_r))
     for b in range(mc):
         g_o2.finish(b)
         norm_rows(out2, mid_all, mo_all, b, 2)
         dsend[o * mc + b] = (0.5 * product(mo_all, b, w_ds)).astype(BF16)
-        for j in range(1, owners):
-            i = b * owners + j
-            ref = dsend.at[o * mc + b]
-            drain.send(ref, ref, dz_s.at[i], dz_r.at[i], grid_peers[j - 1])
+        z_dec.issue(b)
     l_out = load(mo_all.at[f_me], mesh_out)
-    for b in range(mc):
-        for j in near:
-            i = b * owners + j
-            ref = dsend.at[lax.rem(o + owners - j, owners) * mc + b]
-            drain.arrived(ref, dz_s.at[i], dz_r.at[i], grid_peers[j - 1])
-
-    fan = dec_src.shape[1]
+    for source in others:
+        for b in range(mc):
+            z_dec.receive(source, b)
+
+    fan = dec_src.shape[0]
     for g in range(gc):
         sources = []
         for e in range(fan):
-            idx = jnp.clip(dec_src[o * gc + g, e], 0, owners * mc - 1)
+            idx = jnp.clip(dec_src[e, o * gc + g], 0, owners * mc - 1)
             sources.append((lambda rows, idx=idx: dsend[idx, rows, :], None))
 
         def put(rows, value, g=g):
@@ -432,7 +490,7 @@
             squares = squares + stats[f, g, 1:2, :]
         mean = total / d_all
         scale = lax.rsqrt(squares / d_all - mean * mean + EPSILON)
-        value = (dec_out[g] - to_column(mean)) * to_column(scale) * params[3:4, :]
+        value = (dec_out[g] - to_column(mean)) * to_column(scale) * local[0]
         g_stage[g] = (gstate[g].astype(F32) + value).astype(BF16)
         outs.append(load(g_stage.at[g], grid_out.at[g]))
 
@@ -463,17 +521,15 @@
     gr, fin = grid_feat.shape
     mc, gc = mr // BLK, gr // BLK
     depth = enc_send_weight.shape[0]
-    params = jnp.stack(
-        [embed_gain, enc_gain, proc_gain, dec_gain, enc_bias, proc_bias, dec_bias, dec_bias]
-    )
+    vectors = (embed_gain, enc_gain, proc_gain, dec_gain, enc_bias, proc_bias, dec_bias)
     smem = pl.BlockSpec(memory_space=pltpu.SMEM)
-    vmem = pl.BlockSpec(memory_space=pltpu.VMEM)
     hbm = pl.BlockSpec(memory_space=pl.ANY)
     dma = pltpu.SemaphoreType.DMA
     scratch = [pltpu.VMEM((depth, cols), BF16)] * 9
     scratch += [
         pltpu.VMEM((nf, fin, cols), BF16),
-        pltpu.VMEM((nf, 8, cols), F32),
+        pltpu.VMEM((3, nf, 1, cols), F32),
+        pltpu.VMEM((4, 1, cols), F32),
         pltpu.VMEM((nf, mc, BLK, cols), BF16),
         pltpu.VMEM((owners, gr, fin), BF16),
         pltpu.VMEM((nf, fin, cols), BF16),
@@ -497,20 +553,20 @@
         pltpu.VMEM((nf, gc, 8, BLK), F32),
         pltpu.VMEM((gc, BLK, cols), BF16),
     ]
-    scratch += [dma((14 + gc,))]
+    scratch += [dma((20 + gc,))]
     for chunks in (1, 1, mc, mc, mc, mc, gc):
         scratch += gather_sems(chunks, mx, subs)
-    scratch += [dma((owners,))] * 2
+    scratch += [dma((owners + 1,)), dma((owners,))]
     scratch += [dma((owners * mx,))] * 2 + [dma((owners * subs * mx,))] * 2
-    scratch += [dma((nf,))] * 2 + [dma((gc * nf,))] * 2
-    scratch += [dma((2 * mc,))] * 2 + [dma((mc * owners,))] * 2
+    scratch += [dma((3 * nf,))] * 2 + [dma((gc * nf,))] * 2
+    scratch += [dma((2 * mc,))] * 2 + [dma((mc * (owners + 1),)), dma((mc * owners,))]
     grid_out, mesh_out = pl.pallas_call(
         functools.partial(kernel, (owners, mx, subs)),
         out_shape=(
             jax.ShapeDtypeStruct((gc, BLK, cols), BF16),
             jax.ShapeDtypeStruct((mc, BLK, cols), BF16),
         ),
-        in_specs=[smem] * 4 + [vmem] + [hbm] * 12,
+        in_specs=[smem] * 4 + [hbm] * 19,
         out_specs=(hbm, hbm),
         scratch_shapes=scratch,
         compiler_params=pltpu.CompilerParams(
@@ -518,7 +574,7 @@
         ),
         name="graph_step",
     )(
-        enc_src, enc_count.reshape(-1, 1), proc_nbr, dec_src, params, grid_feat,
+        enc_src, enc_count, proc_nbr.T, dec_src.T, *(v.reshape(1, cols) for v in vectors), grid_feat,
         mesh_state.reshape(mc, BLK, cols), embed_weight, enc_send_weight, enc_recv_weight,
         enc_out_weight, proc_send_weight, proc_recv_weight, proc_out_weight, dec_send_weight,
         dec_recv_weight, dec_out_weight,

time: 119 us -> 109 us (0.916); the launches traced: 117 us -> 109 us
  Pallas kernels: 110 us -> 106 us
  local copies, waits for them, and re-layouts: 6.02 us -> 2.59 us
    pallas_call x1, Pallas kernels: 110 us -> 106 us  [on_device(): pl.pallas_call(functools.partial(kernel, (owners, mx, subs)), out_shape=(...]
    unnamed x26 -> x4, local copies, waits for them, and re-layouts: 4.72 us -> 2.59 us
where the time goes in v2:
time: 109 us
  Pallas kernels  106 us (97%)
  local copies, waits for them, and re-layouts  2.59 us (2%)
    pallas_call x1, Pallas kernels, on_device(): pl.pallas_call(functools.partial(kernel, (owners, mx, subs)), out_shape=(...  106 us
    unnamed x4, local copies, waits for them, and re-layouts  2.59 us

profile of v2, /device:TPU:0, one launch (start us, length us, event | category | flops | bytes accessed | tf_op | source)
XLA Modules:
  0.0 109.1 jit_solution(10459533501604406204)
XLA Ops:
  0.6 105.9 %graph_step.1 = (bf16[8,128,256]{2,1,0:T(8,128)(2,1)}, bf16[3,128,256]{2,1,0:T(8,128)(2,1)}) custom-call(s32[12,16]{1,0:T(8,128)} %enc_src.1, s32[12]{0:T(128)} %enc_count.1, s32[6,12]{1,0:T(8,128)} %bitcast.15, s32[3,32]{1,0:T(4,128)} %bitcast.16, f32[1,256]{1,0:T(1,128)} %bitcast.17, f32[1,256]{1,0:T(1,128)} %bitcast.18, f32[1,256]{1,0:T(1,128)} %bitcast.19, ...), custom_call_target="tpu_custom_call" | custom-call | tf_op jit(solution)/shard_map/graph_step/pallas_call | solution.py:563
  106.5 0.0 copy-start
  106.5 1.9 %copy.27 = bf16[1024,256]{1,0:T(8,128)(2,1)} copy(bf16[1024,256]{1,0:T(8,128)(2,1)} %bitcast.12) | data formatting | bytes 1048576
  108.4 0.0 copy-done
  108.4 0.7 copy.28
Async XLA Ops:
  106.5 1.9 %copy-start = (bf16[3,128,256]{2,1,0:T(8,128)(2,1)S(1)}, bf16[3,128,256]{2,1,0:T(8,128)(2,1)}, u32[]{:S(2)}) copy-start(bf16[3,128,256]{2,1,0:T(8,128)(2,1)} %get-tuple-element.5) | copy-start | bytes 589828

commit v3 on v2

--- a/solution.py
+++ b/solution.py
@@ -208,19 +208,9 @@
         return copy
 
     l_we = load(embed_w, we_all.at[f_me])
-    l_es = load(es_w, w_es)
-    l_dr = load(dr_w, w_dr)
-    l_feat = load(grid_feat, feats.at[o])
-    l_ms = load(mesh_state, ms_all.at[f_me])
-    l_er = load(er_w, w_er)
     gain_refs = (e_gain, c_gain, p_gain)
     l_small = [load(ref, gains.at[k, f_me]) for k, ref in enumerate(gain_refs)]
     l_small += [load(ref, local.at[k]) for k, ref in enumerate((d_gain, e_bias, p_bias, d_bias))]
-    l_eo, l_ps, l_pr, l_po, l_ds, l_do = (
-        load(a, b)
-        for a, b in ((eo_w, w_eo), (ps_w, w_ps), (pr_w, w_pr), (po_w, w_po), (ds_w, w_ds), (do_w, w_do))
-    )
-
     feature_peers = []
     for j in range(mx):
         for t in range(subs):
@@ -263,6 +253,17 @@
     z_feat = Line(drain, owners, o, lambda c, _: feats.at[c, part_rows(f_me)], (fz_s, fz_r))
     z_feat.issue(0, grid_feat.at[part_rows(f_me)])
     g_ms.issue(0, mesh_state)
+    l_es = load(es_w, w_es)
+    l_dr = load(dr_w, w_dr)
+    l_feat = load(grid_feat, feats.at[o])
+    l_ms = load(mesh_state, ms_all.at[f_me])
+    l_er, l_eo, l_ps, l_pr, l_po, l_ds, l_do = (
+        load(a, b)
+        for a, b in (
+            (er_w, w_er), (eo_w, w_eo), (ps_w, w_ps), (pr_w, w_pr), (po_w, w_po), (ds_w, w_ds),
+            (do_w, w_do),
+        )
+    )
     g_feat = gather(lambda f, c: feats.at[c, part_rows(f)], (fx_s, fx_r, fs_s, fs_r), owners)
     others = [z_feat.source(i) for i in range(owners - 1)]
 
@@ -368,14 +369,14 @@
         g_h1.issue(b)
 
     def node_layer(g_h, hid, weight, g_o, out):
+        g_h.forward(0)
         for b in range(mc):
-            g_h.forward(b)
-        for b in range(mc):
+            if b + 1 < mc:
+                g_h.forward(b + 1)
             g_h.finish(b)
             out[f_me, b] = product(hid, b, weight).astype(BF16)
             g_o.issue(b)
-        for b in range(mc):
-            g_o.forward(b)
+        g_o.forward(0)
 
     def norm_rows(out, old, new, b, gain_row):
         @pl.loop(0, BLK // SUBROWS)
@@ -402,6 +403,8 @@
     l_ps.wait()
     l_pr.wait()
     for b in range(mc):
+        if b + 1 < mc:
+            g_o1.forward(b + 1)
         g_o1.finish(b)
         norm_rows(out1, ms_all, mid_all, b, 1)
         win[1, b] = (0.5 * product(mid_all, b, w_ps)).astype(BF16)
@@ -432,6 +435,8 @@
     l_ds.wait()
     z_dec = Line(drain, owners, o, lambda c, b: dsend.at[c * mc + b], (dz_s, dz_r))
     for b in range(mc):
+        if b + 1 < mc:
+            g_o2.forward(b + 1)
         g_o2.finish(b)
         norm_rows(out2, mid_all, mo_all, b, 2)
         dsend[o * mc + b] = (0.5 * product(mo_all, b, w_ds)).astype(BF16)

time: 109 us -> 108 us (level)
    pallas_call x1, Pallas kernels: 106 us -> 105 us  [on_device(): pl.pallas_call(functools.partial(kernel, (owners, mx, subs)), out_shape=(...]
where the time goes in v3:
time: 108 us
  Pallas kernels  105 us (97%)
  local copies, waits for them, and re-layouts  2.59 us (2%)
    pallas_call x1, Pallas kernels, on_device(): pl.pallas_call(functools.partial(kernel, (owners, mx, subs)), out_shape=(...  105 us
    unnamed x4, local copies, waits for them, and re-layouts  2.59 us

profile of v3, /device:TPU:0, one launch (start us, length us, event | category | flops | bytes accessed | tf_op | source)
XLA Modules:
  0.0 107.8 jit_solution(5706959247918858350)
XLA Ops:
  0.6 104.5 %graph_step.1 = (bf16[8,128,256]{2,1,0:T(8,128)(2,1)}, bf16[3,128,256]{2,1,0:T(8,128)(2,1)}) custom-call(s32[12,16]{1,0:T(8,128)} %enc_src.1, s32[12]{0:T(128)} %enc_count.1, s32[6,12]{1,0:T(8,128)} %bitcast.15, s32[3,32]{1,0:T(4,128)} %bitcast.16, f32[1,256]{1,0:T(1,128)} %bitcast.17, f32[1,256]{1,0:T(1,128)} %bitcast.18, f32[1,256]{1,0:T(1,128)} %bitcast.19, ...), custom_call_target="tpu_custom_call" | custom-call | tf_op jit(solution)/shard_map/graph_step/pallas_call | solution.py:568
  105.2 0.0 copy-start
  105.2 1.9 %copy.27 = bf16[1024,256]{1,0:T(8,128)(2,1)} copy(bf16[1024,256]{1,0:T(8,128)(2,1)} %bitcast.12) | data formatting | bytes 1048576
  107.1 0.0 copy-done
  107.1 0.7 copy.28
Async XLA Ops:
  105.2 1.9 %copy-start = (bf16[3,128,256]{2,1,0:T(8,128)(2,1)S(1)}, bf16[3,128,256]{2,1,0:T(8,128)(2,1)}, u32[]{:S(2)}) copy-start(bf16[3,128,256]{2,1,0:T(8,128)(2,1)} %get-tuple-element.5) | copy-start | bytes 589828

commit v4 on v3

--- a/solution.py
+++ b/solution.py
@@ -503,10 +503,8 @@
         g_h3.forward(g)
         if g >= 1:
             decode(g - 1)
-        if g >= 3:
-            complete(g - 3)
     decode(gc - 1)
-    for g in range(max(gc - 3, 0), gc):
+    for g in range(gc):
         complete(g)
     l_out.wait()
     for copy in outs:

time: 108 us -> 105 us (0.972)
  Pallas kernels: 105 us -> 102 us
    pallas_call x1, Pallas kernels: 105 us -> 102 us  [on_device(): pl.pallas_call(functools.partial(kernel, (owners, mx, subs)), out_shape=(...]
where the time goes in v4:
time: 105 us
  Pallas kernels  102 us (97%)
  local copies, waits for them, and re-layouts  2.59 us (2%)
    pallas_call x1, Pallas kernels, on_device(): pl.pallas_call(functools.partial(kernel, (owners, mx, subs)), out_shape=(...  102 us
    unnamed x4, local copies, waits for them, and re-layouts  2.59 us

profile of v4, /device:TPU:0, one launch (start us, length us, event | category | flops | bytes accessed | tf_op | source)
XLA Modules:
  0.0 105.0 jit_solution(1125130249258764890)
XLA Ops:
  0.6 101.7 %graph_step.1 = (bf16[8,128,256]{2,1,0:T(8,128)(2,1)}, bf16[3,128,256]{2,1,0:T(8,128)(2,1)}) custom-call(s32[12,16]{1,0:T(8,128)} %enc_src.1, s32[12]{0:T(128)} %enc_count.1, s32[6,12]{1,0:T(8,128)} %bitcast.15, s32[3,32]{1,0:T(4,128)} %bitcast.16, f32[1,256]{1,0:T(1,128)} %bitcast.17, f32[1,256]{1,0:T(1,128)} %bitcast.18, f32[1,256]{1,0:T(1,128)} %bitcast.19, ...), custom_call_target="tpu_custom_call" | custom-call | tf_op jit(solution)/shard_map/graph_step/pallas_call | solution.py:566
  102.4 0.0 copy-start
  102.4 1.9 %copy.27 = bf16[1024,256]{1,0:T(8,128)(2,1)} copy(bf16[1024,256]{1,0:T(8,128)(2,1)} %bitcast.12) | data formatting | bytes 1048576
  104.3 0.0 copy-done
  104.3 0.7 copy.28
Async XLA Ops:
  102.4 1.9 %copy-start = (bf16[3,128,256]{2,1,0:T(8,128)(2,1)S(1)}, bf16[3,128,256]{2,1,0:T(8,128)(2,1)}, u32[]{:S(2)}) copy-start(bf16[3,128,256]{2,1,0:T(8,128)(2,1)} %get-tuple-element.5) | copy-start | bytes 589828
